TPU v7x, 512 devices: a whole 4x8x8 slice. The times are simulated.
512 devices in a mesh: dp: 8 (over y_hi, core), mp: 64 (over z, x, y_lo).
Axes of the slice: x: 4, y: 8 (y_hi: 4, y_lo: 2; y = y_hi * 2 + y_lo), z: 8, core: 2. Of those that a mesh axis runs over, the one named last changes fastest.
Arguments:
- queries: bfloat16 [65536, 768], P(('dp', 'mp')), may hold values from -30 to 30
- first_owner: int32 [65536, 1], P(('dp', 'mp')), may hold values from 0 to 63; in each aligned block of 128 rows (0 to 127, 128 to 255, ...) at most 4 rows name the same one
- first_row: int32 [65536], P(('dp', 'mp')), may hold values from 0 to 255
- tool_table: bfloat16 [16384, 768], P('mp'), may hold values from -6 to 6
- norm_gain: bfloat16 [768], replicated, may hold values from 0.25 to 1.75
- weight_in: bfloat16 [3072, 768], P('mp'), may hold values from -0.21875 to 0.21875
- bias_in: bfloat16 [3072], P('mp'), may hold values from -3 to 3
- weight_out: bfloat16 [3072, 768], P('mp'), may hold values from -0.109375 to 0.109375
- bias_out: bfloat16 [768], replicated, may hold values from -3 to 3
- tool_embeds: bfloat16 [512, 768], P('dp'), may hold values from -2 to 2
- positive: int32 [65536], P(('dp', 'mp')), may hold values from 0 to 511
Outputs:
- updated: bfloat16 [65536, 768], P(('dp', 'mp'))
- chain_loss: float32 [65536], P(('dp', 'mp'))
- query_grad: float32 [65536, 768], P(('dp', 'mp'))
- tool_grad: float32 [512, 768], P('dp')
Inputs may be any that keep to these rules, and one draw needn't show every extreme that they name: `first_owner`: among the 128 chains of one device at most 4 name the same owner, a bound that some block reaches of them.
All inputs are finite; a program needn't handle non-finite values.
Results may differ from a plain program's by a relative error of at most 0.0078.
Values may be sent and summed in bfloat16 or wider, within the bound.
A program may use at most 64 MiB of HBM per device.

v0:
```python
import jax
import jax.numpy as jnp
import numpy as np
from jax import lax
from jax.sharding import PartitionSpec as P


def from_behind(block, axis, distance):
    devices = range(lax.axis_size(axis))
    route = [((i - distance) % len(devices), i) for i in devices]
    return lax.ppermute(block, axis, route)


def layer_normed(combined, norm_gain):
    row_mean = jnp.mean(combined, axis=1, keepdims=True)
    centred = combined - row_mean
    spread = jnp.mean(centred * centred, axis=1, keepdims=True)
    return (centred * lax.rsqrt(spread + 1e-05) * norm_gain.astype(jnp.float32)[None, :]).astype(
        jnp.bfloat16
    )


def hidden_terms(pieces, normed):
    in_piece, bias_piece, out_piece = pieces
    preact = lax.dot_general(
        normed, in_piece, (((1,), (1,)), ((), ())), preferred_element_type=jnp.float32
    )
    preact = preact + bias_piece.astype(jnp.float32)[None, :]
    activated = jax.nn.gelu(preact, approximate=True).astype(jnp.bfloat16)
    return jnp.dot(activated, out_piece, preferred_element_type=jnp.float32)


def local(
    queries,
    first_owner,
    first_row,
    tool_table,
    norm_gain,
    weight_in,
    bias_in,
    weight_out,
    bias_out,
    tool_embeds,
    positive,
):
    chain_count, feature_count = queries.shape
    groups = lax.axis_size("mp")
    cycle_size = lax.axis_size("dp")
    cycle_index = lax.axis_index("dp")
    capacity = 2 * chain_count // groups
    owner_ids = first_owner[:, 0]
    owner_marks = (owner_ids[:, None] == jnp.arange(groups, dtype=jnp.int32)[None, :]).astype(
        jnp.int32
    )
    rank_in_owner = jnp.sum((jnp.cumsum(owner_marks, axis=0) - owner_marks) * owner_marks, axis=1)
    slot_index = owner_ids * capacity + rank_in_owner
    request = (
        jnp.zeros((groups * capacity,), jnp.int32)
        .at[slot_index]
        .set(first_row)
        .reshape(groups, capacity)
    )
    table_rows = jnp.take(
        tool_table, lax.all_to_all(request, "mp", split_axis=0, concat_axis=0, tiled=True), axis=0
    )
    fetched = lax.all_to_all(table_rows, "mp", split_axis=0, concat_axis=0, tiled=True)
    first_rows = fetched.reshape(groups * capacity, feature_count)[slot_index]
    combined = queries.astype(jnp.float32) + first_rows.astype(jnp.float32)
    normed = layer_normed(combined, norm_gain)
    branch_sum = hidden_terms(
        (
            lax.all_gather(weight_in, "mp", axis=0, tiled=True),
            lax.all_gather(bias_in, "mp", axis=0, tiled=True),
            lax.all_gather(weight_out, "mp", axis=0, tiled=True),
        ),
        normed,
    )
    updated = (combined + branch_sum + bias_out.astype(jnp.float32)[None, :]).astype(jnp.bfloat16)
    block_rows = tool_embeds.shape[0]
    forward_hops = cycle_size - 1
    block_list = [tool_embeds]
    offset_list = [0]
    visiting = tool_embeds
    for hop_number in range(forward_hops):
        visiting = from_behind(visiting, "dp", 1)
        block_list.append(visiting)
        offset_list.append(hop_number + 1)
    all_tools = jnp.concatenate(block_list, axis=0)
    block_owner = (cycle_index - jnp.asarray(offset_list, jnp.int32)) % cycle_size
    column_ids = (
        block_owner[:, None] * block_rows + jnp.arange(block_rows, dtype=jnp.int32)[None, :]
    ).reshape(-1)
    scores = lax.dot_general(
        updated, all_tools, (((1,), (1,)), ((), ())), preferred_element_type=jnp.float32
    )
    row_max = jnp.max(scores, axis=1, keepdims=True)
    log_total = row_max + jnp.log(jnp.sum(jnp.exp(scores - row_max), axis=1, keepdims=True))
    is_positive = (column_ids[None, :] == positive[:, None]).astype(jnp.float32)
    chain_loss = log_total[:, 0] - jnp.sum(scores * is_positive, axis=1)
    weights_grad = (jnp.exp(scores - log_total) - is_positive).astype(jnp.bfloat16)
    query_grad = jnp.dot(weights_grad, all_tools, preferred_element_type=jnp.float32)
    position_of = np.zeros((cycle_size,), np.int32)
    for list_index, offset_value in enumerate(offset_list):
        position_of[offset_value] = list_index

    def block_term(offset_value):
        list_index = int(position_of[offset_value])
        columns = weights_grad[:, list_index * block_rows : (list_index + 1) * block_rows]
        return lax.dot_general(
            columns, updated, (((0,), (0,)), ((), ())), preferred_element_type=jnp.float32
        )

    partial_grad = jnp.zeros((block_rows, feature_count), jnp.float32)
    for hop_number in range(cycle_size - 1):
        partial_grad = partial_grad + block_term(hop_number + 1)
        partial_grad = from_behind(partial_grad.astype(jnp.bfloat16), "dp", 1).astype(
            partial_grad.dtype
        )
    partial_grad = partial_grad + block_term(0)
    grad_scale = (block_rows * cycle_size / (chain_count * groups * cycle_size)) ** 0.5
    tool_grad = lax.psum(partial_grad, "mp") * grad_scale
    return (updated, chain_loss, query_grad, tool_grad)


def solution(mesh):
    in_specs = (
        P(("dp", "mp"), None),
        P(("dp", "mp"), None),
        P(("dp", "mp")),
        P("mp", None),
        P(),
        P("mp", None),
        P("mp"),
        P("mp", None),
        P(),
        P("dp", None),
        P(("dp", "mp")),
    )
    out_specs = (P(("dp", "mp"), None), P(("dp", "mp")), P(("dp", "mp"), None), P("dp", None))
    return jax.shard_map(local, mesh=mesh, in_specs=in_specs, out_specs=out_specs, check_vma=False)
```

profile of v0, /device:TPU:16, one launch (start us, length us, event | category | flops | bytes accessed | tf_op | source)
XLA Modules:
  0.0 1266.2 jit_solution(13888815105655201328)
XLA Ops:
  8.0 0.7 all-gather.5.cloned.1.call-update
  8.7 0.7 fusion.20
  9.6 0.8 select_reduce_fusion
  11.1 1.1 scatter_custom_fusion
  12.2 0.7 all_to_all.13
  12.9 14.8 %all-to-all-start = ((s32[64,1,4]{2,1,0:T(1,128)}), s32[64,1,4]{2,1,0:T(1,128)S(1)}, u32[]{:S(2)}, u32[]{:S(2)}) async-start(s32[64,1,4]{2,1,0:T(1,128)} %bitcast.3), calls=%async_computation | async-start | bytes 65536 | tf_op jit(solution)/shard_map/all_to_all | solution.py:64
  27.7 1.9 collective-permute-start
  29.7 1.3 dynamic-slice
  31.6 0.9 dynamic-update-slice
  32.5 0.9 constant_dynamic-update-slice_fusion.7
  33.4 163.7 %all-reduce = bf16[3072]{0:T(1024)(128)(2,1)S(1)} all-reduce(bf16[3072]{0:T(1024)(128)(2,1)S(1)} %dynamic-update-slice), channel_id=1, replica_groups=mesh['dp'=8,'mp'=64] {'mp'}, use_global_device_ids=true, to_apply=%add | all-reduce | flops 3072 | bytes 12288
  198.8 1.2 gather_fusion
  200.1 1.0 broadcast_select_fusion
  201.1 5.3 all-to-all-start.1
  206.5 1.9 collective-permute-start.1
  208.5 6.4 collective-permute-done.1
  214.9 2.1 collective-permute-start.2
  217.0 7.5 collective-permute-done.2
  224.4 1.9 collective-permute-start.3
  226.4 6.5 collective-permute-done.3
  232.9 1.9 collective-permute-start.4
  234.8 5.5 collective-permute-done.4
  240.3 4.1 collective-permute-start.5
  244.4 4.4 collective-permute-done.5
  248.8 3.8 collective-permute-start.6
  252.7 5.0 collective-permute-done.6
  257.8 0.9 gather_fusion.1
  259.1 72.0 %all-gather.3.cloned.1.call-done = bf16[3072,768]{1,0:T(8,128)(2,1)} async-done(((bf16[48,768]{1,0:T(8,128)(2,1)}), bf16[3072,768]{1,0:T(8,128)(2,1)}) %all-gather.3.cloned.1.call-update) | async-done | bytes 4718608 | tf_op jit(solution)/shard_map/all_gather | solution.py:72
  331.1 314.4 %all-gather.5.cloned.1.call-done = bf16[3072,768]{1,0:T(8,128)(2,1)} async-done(((bf16[48,768]{1,0:T(8,128)(2,1)}), bf16[3072,768]{1,0:T(8,128)(2,1)}) %all-gather.5.cloned.1.call-update) | async-done | bytes 4718608 | tf_op jit(solution)/shard_map/all_gather | solution.py:74
  645.5 6.2 fusion.9
  653.4 1.9 collective-permute-start.7
  655.3 5.7 collective-permute-done.7
  661.2 1.9 collective-permute-start.8
  663.4 5.7 collective-permute-done.8
  669.1 1.9 collective-permute-start.9
  671.2 5.8 collective-permute-done.9
  677.0 1.9 collective-permute-start.10
  679.2 5.7 collective-permute-done.10
  684.9 2.1 collective-permute-start.11
  687.2 4.6 collective-permute-done.11
  691.8 3.3 collective-permute-start.12
  695.3 3.3 collective-permute-done.12
  698.6 4.5 collective-permute-start.13
  703.3 2.2 collective-permute-done.13
  705.5 0.7 convert_add_fusion.3
  706.2 1.0 fusion.49
  707.2 550.8 %all-reduce.3.cloned.1.call-done = f32[64,768]{1,0:T(8,128)} async-done(((f32[64,768]{1,0:T(8,128)}), f32[64,768]{1,0:T(8,128)}) %all-reduce.3.cloned.1.call-update) | async-done | bytes 196624 | tf_op jit(solution)/shard_map/psum | solution.py:121
  1258.0 1.6 broadcast_multiply_fusion
  (60 shorter events, 7.2 us)
Async XLA Ops:
  7.2 191.6 %copy-start = (bf16[256,768]{1,0:T(8,128)(2,1)S(1)}, bf16[256,768]{1,0:T(8,128)(2,1)}, u32[]{:S(2)}) copy-start(bf16[256,768]{1,0:T(8,128)(2,1)} %param.15) | copy-start | bytes 1179652
  7.2 323.9 %all-gather.3.cloned.1.call-start = ((), (), s32[]{:S(2)}) async-start(), calls=%async_computation.2 | async-start | bytes 4792320 | tf_op jit(solution)/shard_map/all_gather | solution.py:72
  7.9 637.6 %all-gather.5.cloned.1.call-start = ((), (), s32[]{:S(2)}) async-start(), calls=%async_computation.3 | async-start | bytes 4792320 | tf_op jit(solution)/shard_map/all_gather | solution.py:74
  12.9 185.7 %all-to-all-start = ((s32[64,1,4]{2,1,0:T(1,128)}), s32[64,1,4]{2,1,0:T(1,128)S(1)}, u32[]{:S(2)}, u32[]{:S(2)}) async-start(s32[64,1,4]{2,1,0:T(1,128)} %bitcast.3), calls=%async_computation | async-start | bytes 65536 | tf_op jit(solution)/shard_map/all_to_all | solution.py:64
  27.7 178.8 %collective-permute-start = (bf16[64,768]{1,0:T(8,128)(2,1)}, bf16[64,768]{1,0:T(8,128)(2,1)S(1)}, u32[]{:S(2)}, u32[]{:S(2)}) collective-permute-start(bf16[64,768]{1,0:T(8,128)(2,1)} %param.21), channel_id=1, source_target_pairs={{448,0},{0,64},{64,128},{128,192},{192,256},{256,320},{320,384},{3... | collective-permute-start | bytes 294920 | tf_op jit(solution)/shard_map/ppermute | solution.py:11
  201.1 56.6 %all-to-all-start.1 = ((bf16[64,4,768]{2,1,0:T(4,128)(2,1)}), bf16[64,4,768]{2,1,0:T(4,128)(2,1)S(1)}, u32[]{:S(2)}, u32[]{:S(2)}) async-start(bf16[64,4,768]{2,1,0:T(4,128)(2,1)} %broadcast_select_fusion), calls=%async_computation.1 | async-start | bytes 786432 | tf_op jit(solution)/shard_map/all_to_all | solution.py:66
  206.5 1051.5 %all-reduce.3.cloned.1.call-start = ((), (), s32[]{:S(2)}) async-start(), calls=%async_computation.4 | async-start | bytes 393216 | tf_op jit(solution)/shard_map/psum | solution.py:121
  206.5 8.4 collective-permute-start.1
  214.9 9.5 collective-permute-start.2
  224.4 8.4 collective-permute-start.3
  232.9 7.4 collective-permute-start.4
  234.8 23.9 %copy-start.2 = (bf16[128,768]{1,0:T(8,128)(2,1)S(1)}, bf16[128,768]{1,0:T(8,128)(2,1)}, u32[]{:S(2)}) copy-start(bf16[128,768]{1,0:T(8,128)(2,1)} %param.12) | copy-start | bytes 589828
  240.3 8.5 collective-permute-start.5
  248.8 8.9 collective-permute-start.6
  259.0 393.2 %copy-start.3 = (s32[128]{0:T(128)S(1)}, s32[128]{0:T(128)}, u32[]{:S(2)}) copy-start(s32[128]{0:T(128)} %param.22) | copy-start | bytes 1540
  651.7 51.4 %copy-start.1 = (bf16[128,768]{1,0:T(8,128)(2,1)}, bf16[128,768]{1,0:T(8,128)(2,1)S(1)}, u32[]{:S(2)}) copy-start(bf16[128,768]{1,0:T(8,128)(2,1)S(1)} %fusion.9) | copy-start | bytes 589828
  653.4 7.6 collective-permute-start.7
  661.2 7.9 collective-permute-start.8
  669.1 7.9 collective-permute-start.9
  677.0 7.9 collective-permute-start.10
  684.9 6.8 collective-permute-start.11
  691.8 6.8 collective-permute-start.12
  698.6 6.8 collective-permute-start.13
Sparse Core Ops, SparseCore 0:
  10.1 320.9 all-gather.2
  333.2 312.3 all-gather.4
  706.3 551.6 all-reduce.2
where the time goes:
time: 1270 us
  waiting for transfers between devices  1010 us (80%)
  blocking collectives  164 us (13%)
  starting transfers between devices  55.3 us (4%)
  between operations  14.9 us (1%)
    psum x1, waiting for transfers between devices, local(): tool_grad = lax.psum(partial_grad, 'mp') * grad_scale  551 us
    all_gather x1, waiting for transfers between devices, local(): lax.all_gather(weight_out, 'mp', axis=0, tiled=True)  314 us
    unnamed x1, blocking collectives  164 us
    all_gather x1, waiting for transfers between devices, local(): lax.all_gather(weight_in, 'mp', axis=0, tiled=True)  72 us
    ppermute x14, waiting for transfers between devices, from_behind(): return lax.ppermute(block, axis, route)  68.2 us
    ppermute x14, starting transfers between devices, from_behind(): return lax.ppermute(block, axis, route)  35.1 us
  transfers between devices with their start and end apart: 19, of which 16 were waited for; matrix products, arithmetic and copies ran while one was open for 1% of the time, Pallas kernels for 0%

commit v1 on v0

--- a/solution.py
+++ b/solution.py
@@ -3,6 +3,7 @@
 import numpy as np
 from jax import lax
 from jax.sharding import PartitionSpec as P
+from jax.lax import all_to_all, axis_size
 
 
 def from_behind(block, axis, distance):
@@ -67,9 +68,18 @@
     first_rows = fetched.reshape(groups * capacity, feature_count)[slot_index]
     combined = queries.astype(jnp.float32) + first_rows.astype(jnp.float32)
     normed = layer_normed(combined, norm_gain)
+    _do_widths = lambda sheet, across: jnp.concatenate(
+        all_to_all(
+            jnp.stack([sheet for _ in range(axis_size(across))]),
+            across,
+            concat_axis=0,
+            split_axis=0,
+        ),
+        axis=0,
+    )
     branch_sum = hidden_terms(
         (
-            lax.all_gather(weight_in, "mp", axis=0, tiled=True),
+            _do_widths(weight_in, "mp"),
             lax.all_gather(bias_in, "mp", axis=0, tiled=True),
             lax.all_gather(weight_out, "mp", axis=0, tiled=True),
         ),

time: 1270 us -> 1010 us (0.80)
  waiting for transfers between devices: 1010 us -> 641 us
  blocking collectives: 164 us -> 267 us
    all_gather x1, waiting for transfers between devices: 314 us -> 49.5 us  [local(): lax.all_gather(weight_out, 'mp', axis=0, tiled=True)]
    all_gather x1 -> x0, waiting for transfers between devices: 72 us -> none  [local(): lax.all_gather(weight_in, 'mp', axis=0, tiled=True)]
    unnamed x1, blocking collectives: 164 us -> 223 us
    all_to_all x0 -> x2, blocking collectives: none -> 43.4 us  [the longest x1 25 us: local(): lax.all_to_all(request, 'mp', split_axis=0, concat_axis=0, tiled=True)]
    ppermute x14, waiting for transfers between devices: 68.2 us -> 38.1 us  [from_behind(): return lax.ppermute(block, axis, route)]
    ppermute x14, starting transfers between devices: 35.1 us -> 59.7 us  [from_behind(): return lax.ppermute(block, axis, route)]
    all_to_all x2 -> x1, starting transfers between devices: 20.1 us -> 5.83 us  [local(): all_to_all(jnp.stack([sheet for _ in range(axis_size(across))]), across,...]
  transfers between devices with their start and end apart: 19 -> 17, of which waited for: 16 -> 15; matrix products, arithmetic and copies ran while one was open for 1% -> 1% of each run, Pallas kernels for 0% -> 0%
where the time goes in v1:
time: 1010 us
  waiting for transfers between devices  641 us (63%)
  blocking collectives  267 us (26%)
  starting transfers between devices  65.6 us (6%)
  between operations  15.2 us (2%)
    psum x1, waiting for transfers between devices, local(): tool_grad = lax.psum(partial_grad, 'mp') * grad_scale  553 us
    unnamed x1, blocking collectives  223 us
    ppermute x14, starting transfers between devices, from_behind(): return lax.ppermute(block, axis, route)  59.7 us
    all_gather x1, waiting for transfers between devices, local(): lax.all_gather(weight_out, 'mp', axis=0, tiled=True)  49.5 us
    ppermute x14, waiting for transfers between devices, from_behind(): return lax.ppermute(block, axis, route)  38.1 us
    all_to_all x1, blocking collectives, local(): lax.all_to_all(request, 'mp', split_axis=0, concat_axis=0, tiled=True)  25 us
  transfers between devices with their start and end apart: 17, of which 15 were waited for; matrix products, arithmetic and copies ran while one was open for 1% of the time, Pallas kernels for 0%

profile of v1, /device:TPU:16, one launch (start us, length us, event | category | flops | bytes accessed | tf_op | source)
XLA Modules:
  0.0 1012.6 jit_solution(16988291936560571691)
XLA Ops:
  7.2 0.8 fusion.20
  8.1 0.8 select_reduce_fusion
  9.0 0.7 fusion.40
  9.6 1.1 scatter_custom_fusion
  10.9 25.0 %all_to_all.25 = s32[64,1,4]{2,1,0:T(1,128)S(1)} all-to-all(s32[64,1,4]{2,1,0:T(1,128)S(1)} %bitcast.30), channel_id=1, replica_groups=mesh['dp'=8,'mp'=64] {'mp'}, dimensions={0} | all-to-all | bytes 2048 | tf_op jit(solution)/shard_map/all_to_all | solution.py:65
  36.0 1.2 gather_fusion
  37.6 18.4 %all_to_all.26 = bf16[64,4,768]{2,1,0:T(4,128)(2,1)S(1)} all-to-all(bf16[64,4,768]{2,1,0:T(4,128)(2,1)S(1)} %broadcast_select_fusion), channel_id=1, replica_groups=mesh['dp'=8,'mp'=64] {'mp'}, dimensions={0} | all-to-all | bytes 786432 | tf_op jit(solution)/shard_map/all_to_all | solution.py:67
  56.0 2.5 stack.2
  58.6 5.8 all-to-all-start.2
  64.5 0.7 all-gather.2.cloned.1.call-update
  65.2 1.9 collective-permute-start
  67.1 1.3 dynamic-slice
  69.3 223.4 %all-reduce = bf16[3072]{0:T(1024)(128)(2,1)S(1)} all-reduce(bf16[3072]{0:T(1024)(128)(2,1)S(1)} %dynamic-update-slice), channel_id=1, replica_groups=mesh['dp'=8,'mp'=64] {'mp'}, use_global_device_ids=true, to_apply=%add | all-reduce | flops 3072 | bytes 12288
  293.0 1.9 collective-permute-start.1
  294.9 4.9 collective-permute-done.1
  299.8 1.9 collective-permute-start.2
  301.8 6.0 collective-permute-done.2
  307.8 2.8 collective-permute-start.3
  310.5 5.0 collective-permute-done.3
  315.5 3.6 collective-permute-start.4
  319.1 3.6 collective-permute-done.4
  322.7 4.6 collective-permute-start.5
  327.4 3.2 collective-permute-done.5
  330.6 6.5 collective-permute-start.6
  337.1 2.0 collective-permute-done.6
  339.1 0.9 gather_fusion.1
  340.4 49.5 %all-gather.2.cloned.1.call-done = bf16[3072,768]{1,0:T(8,128)(2,1)} async-done(((bf16[48,768]{1,0:T(8,128)(2,1)}), bf16[3072,768]{1,0:T(8,128)(2,1)}) %all-gather.2.cloned.1.call-update) | async-done | bytes 4718608 | tf_op jit(solution)/shard_map/all_gather | solution.py:84
  389.9 6.2 fusion.9
  396.1 0.5 fusion.48
  396.8 0.5 fusion.47
  397.7 1.9 collective-permute-start.7
  399.7 4.9 collective-permute-done.7
  404.8 3.1 collective-permute-start.8
  408.2 3.5 collective-permute-done.8
  411.7 4.5 collective-permute-start.9
  416.3 2.2 collective-permute-done.9
  418.5 5.8 collective-permute-start.10
  424.6 0.8 collective-permute-done.10
  425.4 7.0 collective-permute-start.11
  432.6 0.7 collective-permute-done.11
  433.3 7.1 collective-permute-start.12
  440.7 0.7 collective-permute-done.12
  441.4 7.1 collective-permute-start.13
  448.7 0.7 collective-permute-done.13
  449.4 0.7 convert_add_fusion.3
  450.2 1.0 fusion.49
  451.2 552.9 %all-reduce.3.cloned.1.call-done = f32[64,768]{1,0:T(8,128)} async-done(((f32[64,768]{1,0:T(8,128)}), f32[64,768]{1,0:T(8,128)}) %all-reduce.3.cloned.1.call-update) | async-done | bytes 196624 | tf_op jit(solution)/shard_map/psum | solution.py:131
  1004.1 1.6 broadcast_multiply_fusion
  (68 shorter events, 4.1 us)
Async XLA Ops:
  7.2 28.9 %copy-start = (bf16[256,768]{1,0:T(8,128)(2,1)S(1)}, bf16[256,768]{1,0:T(8,128)(2,1)}, u32[]{:S(2)}) copy-start(bf16[256,768]{1,0:T(8,128)(2,1)} %param.15) | copy-start | bytes 1179652
  37.2 18.8 %copy-start.4 = (bf16[48,768]{1,0:T(8,128)(2,1)S(1)}, bf16[48,768]{1,0:T(8,128)(2,1)}, u32[]{:S(2)}) copy-start(bf16[48,768]{1,0:T(8,128)(2,1)} %param.17) | copy-start | bytes 221188
  58.6 6.6 copy-start.3
  58.6 10.5 %copy-start.8 = (bf16[48]{0:T(256)(128)(2,1)S(1)}, bf16[48]{0:T(256)(128)(2,1)}, u32[]{:S(2)}) copy-start(bf16[48]{0:T(256)(128)(2,1)} %param.18) | copy-start | bytes 292
  58.6 234.2 %copy-start.6 = (bf16[768]{0:T(1024)(128)(2,1)S(1)}, bf16[768]{0:T(1024)(128)(2,1)}, u32[]{:S(2)}) copy-start(bf16[768]{0:T(1024)(128)(2,1)} %param.16) | copy-start | bytes 4612
  58.6 234.2 %copy-start.7 = (bf16[768]{0:T(1024)(128)(2,1)S(1)}, bf16[768]{0:T(1024)(128)(2,1)}, u32[]{:S(2)}) copy-start(bf16[768]{0:T(1024)(128)(2,1)} %param.20) | copy-start | bytes 4612
  58.6 281.8 %all-to-all-start.2 = ((bf16[64,48,768]{2,1,0:T(8,128)(2,1)}), bf16[64,48,768]{2,1,0:T(8,128)(2,1)}, u32[]{:S(2)}, u32[]{:S(2)}) async-start(bf16[64,48,768]{2,1,0:T(8,128)(2,1)} %stack.2), calls=%async_computation.2 | async-start | bytes 9437184 | tf_op jit(solution)/shard_map/all_to_all | solution.py:72
  64.4 325.5 %all-gather.2.cloned.1.call-start = ((), (), s32[]{:S(2)}) async-start(), calls=%async_computation.3 | async-start | bytes 4792320 | tf_op jit(solution)/shard_map/all_gather | solution.py:84
  65.2 939.0 %all-reduce.3.cloned.1.call-start = ((), (), s32[]{:S(2)}) async-start(), calls=%async_computation.4 | async-start | bytes 393216 | tf_op jit(solution)/shard_map/psum | solution.py:131
  65.2 227.8 %collective-permute-start = (bf16[64,768]{1,0:T(8,128)(2,1)S(1)}, bf16[64,768]{1,0:T(8,128)(2,1)S(1)}, u32[]{:S(2)}, u32[]{:S(2)}) collective-permute-start(bf16[64,768]{1,0:T(8,128)(2,1)S(1)} %copy-done.3), channel_id=1, source_target_pairs={{448,0},{0,64},{64,128},{128,192},{192,256},{256,320},{320,384},{3... | collective-permute-start | bytes 294920 | tf_op jit(solution)/shard_map/ppermute | solution.py:12
  293.0 6.8 collective-permute-start.1
  299.8 7.9 collective-permute-start.2
  307.8 7.8 collective-permute-start.3
  315.5 7.2 collective-permute-start.4
  319.1 20.9 %copy-start.2 = (bf16[128,768]{1,0:T(8,128)(2,1)S(1)}, bf16[128,768]{1,0:T(8,128)(2,1)}, u32[]{:S(2)}) copy-start(bf16[128,768]{1,0:T(8,128)(2,1)} %param.12) | copy-start | bytes 589828
  322.7 7.8 collective-permute-start.5
  330.6 8.5 collective-permute-start.6
  389.9 6.7 copy-start.5
  396.1 52.4 %copy-start.1 = (bf16[128,768]{1,0:T(8,128)(2,1)}, bf16[128,768]{1,0:T(8,128)(2,1)S(1)}, u32[]{:S(2)}) copy-start(bf16[128,768]{1,0:T(8,128)(2,1)S(1)} %fusion.9) | copy-start | bytes 589828
  397.7 6.9 collective-permute-start.7
  404.8 6.8 collective-permute-start.8
  411.7 6.8 collective-permute-start.9
  418.5 6.8 collective-permute-start.10
  425.4 7.9 collective-permute-start.11
  433.3 8.0 collective-permute-start.12
  441.4 8.0 collective-permute-start.13
Sparse Core Ops, SparseCore 0:
  67.3 322.5 all-gather.1
  450.3 553.8 all-reduce.2
